TPU v7x, 1024 devices: a whole 8x8x8 slice. The times are simulated.
1024 devices in a mesh: seq: 128 (over x, y, core), head: 8 (over z).
Axes of the slice: x: 8, y: 8, z: 8, core: 2. Of those that a mesh axis runs over, the one named last changes fastest.
Arguments:
- queries: bfloat16 [16384, 8192], P('seq', 'head'), parts along dimension 1, may hold values from -12 to 12
- key_rows: bfloat16 [16384, 1024], P('seq', 'head'), parts along dimension 1, may hold values from -12 to 12
- value_rows: bfloat16 [16384, 1024], P('seq', 'head'), parts along dimension 1, may hold values from -6 to 6
- out_grad: bfloat16 [16384, 8192], P('seq', 'head'), parts along dimension 1, may hold values from -6 to 6
- doc_blocks: int32 [64], replicated, may hold values from 1 to 8, 128 in all
Outputs:
- attended: bfloat16 [16384, 8192], P('seq', 'head'), parts along dimension 1
- query_grad: bfloat16 [16384, 8192], P('seq', 'head'), parts along dimension 1
- key_grad: bfloat16 [16384, 1024], P('seq', 'head'), parts along dimension 1
- value_grad: bfloat16 [16384, 1024], P('seq', 'head'), parts along dimension 1
There are 8 independent parts, one for each index of `head`. A program takes and returns all parts, laid end to end along the dimension named above; an argument that names none is the same for every part. Nothing has to cross between parts.
All inputs are finite; a program needn't handle non-finite values.
Results may differ from a plain program's by a relative error of at most 0.013.
Values may be sent and summed in bfloat16 or wider, within the bound.
A program may use at most 32 MiB of HBM per device.

v0:
```python
import jax
import jax.numpy as jnp
from jax import lax
from jax.sharding import PartitionSpec as P

BLOCK = 128


def shifted(value, axis, steps):
    count = lax.axis_size(axis)
    first, last = (max(0, -steps), min(count, count - steps))
    return lax.ppermute(value, axis, [(source, source + steps) for source in range(first, last)])


def doc_index(positions, ends):
    return jnp.sum((ends[None, :] <= positions[:, None]).astype(jnp.int32), axis=1)


def local(queries, key_rows, value_rows, out_grad, doc_blocks):
    row_count = queries.shape[0]
    head_width = key_rows.shape[1]
    head_count = queries.shape[1] // head_width
    window = min(8, lax.axis_size("seq") // 2)
    score_scale = head_width ** (-0.5)
    device_index = lax.axis_index("seq")
    joined = jnp.concatenate([key_rows, value_rows], axis=1)

    def advance(turn_index, carried):
        current, stored_rows = carried
        current = shifted(current, "seq", 1)
        stored_rows = lax.dynamic_update_slice(stored_rows, current[None], (turn_index, 0, 0))
        return (current, stored_rows)

    stored = jnp.zeros((window, row_count, 2 * head_width), jnp.bfloat16).at[0].set(joined)
    stored = lax.fori_loop(1, window, advance, (joined, stored))[1]
    tile_rows = 2 * row_count
    tile_count = window // 2
    tiles_kv = stored.reshape(tile_count, tile_rows, 2 * head_width)
    ends = BLOCK * jnp.cumsum(doc_blocks)
    query_pos = device_index * row_count + jnp.arange(row_count, dtype=jnp.int32)
    row_pos = jnp.repeat(query_pos, head_count)
    row_doc = doc_index(row_pos, ends)
    window_rows = jnp.arange(window * row_count, dtype=jnp.int32)
    key_pos = (device_index - window_rows // row_count) * row_count + window_rows % row_count
    key_doc = doc_index(key_pos, ends)
    tiles_pos = key_pos.reshape(tile_count, tile_rows)
    tiles_doc = key_doc.reshape(tile_count, tile_rows)
    rows_query = queries.reshape(row_count * head_count, head_width)
    rows_grad = out_grad.reshape(row_count * head_count, head_width)
    contract_last = (((1,), (1,)), ((), ()))
    contract_first = (((0,), (0,)), ((), ()))

    def tile_scores(key_tile, tile_pos, tile_doc):
        scores = (
            lax.dot_general(rows_query, key_tile, contract_last, preferred_element_type=jnp.float32)
            * score_scale
        )
        allowed = (
            (tile_pos[None, :] >= 0)
            & (tile_pos[None, :] <= row_pos[:, None])
            & (tile_doc[None, :] == row_doc[:, None])
        )
        return (scores, allowed)

    def stats_step(carried, tile_item):
        running_max, running_sum = carried
        kv_tile, tile_pos, tile_doc = tile_item
        scores, allowed = tile_scores(kv_tile[:, :head_width], tile_pos, tile_doc)
        new_max = jnp.maximum(running_max, jnp.max(jnp.where(allowed, scores, -1e30), axis=1))
        tile_sum = jnp.sum(jnp.where(allowed, jnp.exp(scores - new_max[:, None]), 0.0), axis=1)
        running_sum = running_sum * jnp.exp(running_max - new_max) + tile_sum
        return ((new_max, running_sum), None)

    start_max = jnp.full((row_count * head_count,), -1e30, jnp.float32)
    start_sum = jnp.zeros((row_count * head_count,), jnp.float32)
    tile_items = (tiles_kv, tiles_pos, tiles_doc)
    (final_max, final_sum), unused = lax.scan(stats_step, (start_max, start_sum), tile_items)
    lse = final_max + jnp.log(final_sum)

    def tile_weights(kv_tile, tile_pos, tile_doc):
        scores, allowed = tile_scores(kv_tile[:, :head_width], tile_pos, tile_doc)
        return jnp.where(allowed, jnp.exp(scores - lse[:, None]), 0.0)

    def output_step(accumulated, tile_item):
        kv_tile, tile_pos, tile_doc = tile_item
        weights_bf = tile_weights(kv_tile, tile_pos, tile_doc).astype(jnp.bfloat16)
        accumulated = accumulated + jnp.dot(
            weights_bf, kv_tile[:, head_width:], preferred_element_type=jnp.float32
        )
        return (accumulated, None)

    start_rows = jnp.zeros((row_count * head_count, head_width), jnp.float32)
    attended_rows = lax.scan(output_step, start_rows, tile_items)[0].astype(jnp.bfloat16)
    delta = jnp.sum(rows_grad.astype(jnp.float32) * attended_rows.astype(jnp.float32), axis=1)

    def backward_step(accumulated, tile_item):
        kv_tile, tile_pos, tile_doc = tile_item
        weights = tile_weights(kv_tile, tile_pos, tile_doc)
        weights_bf = weights.astype(jnp.bfloat16)
        grad_weights = lax.dot_general(
            rows_grad, kv_tile[:, head_width:], contract_last, preferred_element_type=jnp.float32
        )
        grad_scores = (weights * (grad_weights - delta[:, None]) * score_scale).astype(jnp.bfloat16)
        accumulated = accumulated + jnp.dot(
            grad_scores, kv_tile[:, :head_width], preferred_element_type=jnp.float32
        )
        key_part = lax.dot_general(
            grad_scores, rows_query, contract_first, preferred_element_type=jnp.float32
        )
        value_part = lax.dot_general(
            weights_bf, rows_grad, contract_first, preferred_element_type=jnp.float32
        )
        return (accumulated, jnp.concatenate([key_part, value_part], axis=1))

    query_rows_grad, tile_parts = lax.scan(backward_step, start_rows, tile_items)
    partials = tile_parts.reshape(window, row_count, 2 * head_width)

    def carry_back(turn_index, running_grads):
        source = window - 2 - turn_index
        moved = shifted(running_grads.astype(jnp.bfloat16), "seq", -1).astype(running_grads.dtype)
        return moved + lax.dynamic_index_in_dim(partials, source, 0, keepdims=False)

    grads = lax.fori_loop(0, window - 1, carry_back, partials[window - 1])
    attended = attended_rows.reshape(row_count, head_count * head_width)
    query_grad = query_rows_grad.astype(jnp.bfloat16).reshape(row_count, head_count * head_width)
    key_grad = grads[:, :head_width].astype(jnp.bfloat16)
    value_grad = grads[:, head_width:].astype(jnp.bfloat16)
    return (attended, query_grad, key_grad, value_grad)


def solution(mesh):
    in_specs = (P("seq", "head"), P("seq", "head"), P("seq", "head"), P("seq", "head"), P())
    out_specs = (P("seq", "head"), P("seq", "head"), P("seq", "head"), P("seq", "head"))
    return jax.shard_map(local, mesh=mesh, in_specs=in_specs, out_specs=out_specs, check_vma=False)
```

profile of v0, /device:TPU:503, one launch (start us, length us, event | category | flops | bytes accessed | tf_op | source)
XLA Modules:
  0.0 147.9 jit_solution(4540191611396769647)
XLA Ops:
  4.7 58.2 %while.68 = (s32[]{:T(128)}, bf16[128,256]{1,0:T(8,128)(2,1)S(1)}, bf16[8,128,256]{2,1,0:T(8,128)(2,1)S(1)}, s32[]{:T(128)}, s32[]{:T(128)}, /*index=5*/s32[]{:T(128)}) while((s32[]{:T(128)}, bf16[128,256]{1,0:T(8,128)(2,1)S(1)}, bf16[8,128,256]{2,1,0:T(8,128)(2,1)S(1)}, s32[]{:T(128)}, s32[]{:T(128)}, /*index=5*/s32[]{:T(128)}) %tuple.133), condition=%wide.region_1.0_spmd, body=%wide.region_0.0_spmd.sunk | while | flops 5 | bytes 524435 | solution.py:35
  4.7 3.3 %collective-permute-start = (bf16[128,256]{1,0:T(8,128)(2,1)S(1)}, bf16[128,256]{1,0:T(8,128)(2,1)S(1)}, u32[]{:S(2)}, u32[]{:S(2)}) collective-permute-start(bf16[128,256]{1,0:T(8,128)(2,1)S(1)} %get-tuple-element.771), channel_id=1, source_target_pairs={{0,8},{8,16},{16,24},{24,32},{32,40},{40,48},{48,56},{56,64},{64,7... | collective-permute-start | bytes 196616 | tf_op jit(solution)/shard_map/while/body/eval_jaxpr/ppermute | solution.py:12
  8.0 1.3 collective-permute-done
  9.3 7.6 %collective-permute-start = (bf16[128,256]{1,0:T(8,128)(2,1)S(1)}, bf16[128,256]{1,0:T(8,128)(2,1)S(1)}, u32[]{:S(2)}, u32[]{:S(2)}) collective-permute-start(bf16[128,256]{1,0:T(8,128)(2,1)S(1)} %get-tuple-element.771), channel_id=1, source_target_pairs={{0,8},{8,16},{16,24},{24,32},{32,40},{40,48},{48,56},{56,64},{64,7... | collective-permute-start | bytes 196616 | tf_op jit(solution)/shard_map/while/body/eval_jaxpr/ppermute | solution.py:12
  16.9 1.3 collective-permute-done
  18.2 7.6 %collective-permute-start = (bf16[128,256]{1,0:T(8,128)(2,1)S(1)}, bf16[128,256]{1,0:T(8,128)(2,1)S(1)}, u32[]{:S(2)}, u32[]{:S(2)}) collective-permute-start(bf16[128,256]{1,0:T(8,128)(2,1)S(1)} %get-tuple-element.771), channel_id=1, source_target_pairs={{0,8},{8,16},{16,24},{24,32},{32,40},{40,48},{48,56},{56,64},{64,7... | collective-permute-start | bytes 196616 | tf_op jit(solution)/shard_map/while/body/eval_jaxpr/ppermute | solution.py:12
  25.8 1.3 collective-permute-done
  27.2 7.6 %collective-permute-start = (bf16[128,256]{1,0:T(8,128)(2,1)S(1)}, bf16[128,256]{1,0:T(8,128)(2,1)S(1)}, u32[]{:S(2)}, u32[]{:S(2)}) collective-permute-start(bf16[128,256]{1,0:T(8,128)(2,1)S(1)} %get-tuple-element.771), channel_id=1, source_target_pairs={{0,8},{8,16},{16,24},{24,32},{32,40},{40,48},{48,56},{56,64},{64,7... | collective-permute-start | bytes 196616 | tf_op jit(solution)/shard_map/while/body/eval_jaxpr/ppermute | solution.py:12
  34.8 1.3 collective-permute-done
  36.1 7.6 %collective-permute-start = (bf16[128,256]{1,0:T(8,128)(2,1)S(1)}, bf16[128,256]{1,0:T(8,128)(2,1)S(1)}, u32[]{:S(2)}, u32[]{:S(2)}) collective-permute-start(bf16[128,256]{1,0:T(8,128)(2,1)S(1)} %get-tuple-element.771), channel_id=1, source_target_pairs={{0,8},{8,16},{16,24},{24,32},{32,40},{40,48},{48,56},{56,64},{64,7... | collective-permute-start | bytes 196616 | tf_op jit(solution)/shard_map/while/body/eval_jaxpr/ppermute | solution.py:12
  43.7 1.3 collective-permute-done
  45.0 7.6 %collective-permute-start = (bf16[128,256]{1,0:T(8,128)(2,1)S(1)}, bf16[128,256]{1,0:T(8,128)(2,1)S(1)}, u32[]{:S(2)}, u32[]{:S(2)}) collective-permute-start(bf16[128,256]{1,0:T(8,128)(2,1)S(1)} %get-tuple-element.771), channel_id=1, source_target_pairs={{0,8},{8,16},{16,24},{24,32},{32,40},{40,48},{48,56},{56,64},{64,7... | collective-permute-start | bytes 196616 | tf_op jit(solution)/shard_map/while/body/eval_jaxpr/ppermute | solution.py:12
  52.6 1.3 collective-permute-done
  54.0 7.6 %collective-permute-start = (bf16[128,256]{1,0:T(8,128)(2,1)S(1)}, bf16[128,256]{1,0:T(8,128)(2,1)S(1)}, u32[]{:S(2)}, u32[]{:S(2)}) collective-permute-start(bf16[128,256]{1,0:T(8,128)(2,1)S(1)} %get-tuple-element.771), channel_id=1, source_target_pairs={{0,8},{8,16},{16,24},{24,32},{32,40},{40,48},{48,56},{56,64},{64,7... | collective-permute-start | bytes 196616 | tf_op jit(solution)/shard_map/while/body/eval_jaxpr/ppermute | solution.py:12
  62.9 5.0 %while.70 = (s32[]{:T(128)}, f32[1024]{0:T(1024)S(1)}, f32[1024]{0:T(1024)S(1)}, s32[4,256]{1,0:T(4,128)S(1)}, s32[4,256]{1,0:T(4,128)S(1)}, /*index=5*/s32[1024...) while((s32[]{:T(128)}, f32[1024]{0:T(1024)S(1)}, ...), condition=%wide.region_8.9_spmd.clone, body=%wide.region_5.8_spmd.clone.sunk | while | flops 70784256 | bytes 2778764 | solution.py:77
  68.0 4.5 %while.71 = (s32[]{:T(128)}, f32[1024,128]{1,0:T(8,128)S(1)}, s32[4,256]{1,0:T(4,128)S(1)}, s32[4,256]{1,0:T(4,128)S(1)}, s32[1024]{0:T(1024)S(1)}, /*index=5*/b...) while((s32[]{:T(128)}, f32[1024,128]{1,0:T(8,128)S(1)}, ...), condition=%wide.region_10.11_spmd.clone, body=%wide.region_9.10_spmd.clone.sunk | while | flops 136577280 | bytes 1735819 | solution.py:93
  73.5 9.7 %while.72 = (s32[]{:T(128)}, f32[1024,128]{1,0:T(8,128)S(1)}, f32[4,256,256]{2,1,0:T(8,128)S(1)}, s32[4,256]{1,0:T(4,128)S(1)}, s32[4,256]{1,0:T(4,128)S(1)}, /*...) while((s32[]{:T(128)}, f32[1024,128]{1,0:T(8,128)S(1)}, ...), condition=%wide.region_13.14_spmd.clone, body=%wide.region_12.13_spmd.clone.sunk | while | flops 339017984 | bytes 9145767 | solution.py:115
  83.3 63.2 %while.69 = (s32[]{:T(128)}, bf16[128,256]{1,0:T(8,128)(2,1)S(1)}, f32[8,128,256]{2,1,0:T(8,128)S(1)}, s32[]{:T(128)}, s32[]{:T(128)}, /*index=5*/s32[]{:T(128)}, s32[]{:T(128)}) while((s32[]{:T(128)}, bf16[128,256]{1,0:T(8,128)(2,1)S(1)}, f32[8,128,256]{2,1,0:T(8,128)S(1)}, s32[]{:T(128)}, s32[]{:T(128)}, /*index=5*/s32[]{:T(128)}, ...), condition=%wide.region_15.16_spmd, body=%wide.region_14.15_spmd.sunk | while | flops 98310 | bytes 524463 | solution.py:123
  83.3 1.9 %collective-permute-start.1 = (bf16[128,256]{1,0:T(8,128)(2,1)S(1)}, bf16[128,256]{1,0:T(8,128)(2,1)S(1)}, u32[]{:S(2)}, u32[]{:S(2)}) collective-permute-start(bf16[128,256]{1,0:T(8,128)(2,1)S(1)} %get-tuple-element.898), channel_id=1, source_target_pairs={{8,0},{16,8},{24,16},{32,24},{40,32},{48,40},{56,48},{64,56},{72,6... | collective-permute-start | bytes 196616 | tf_op jit(solution)/shard_map/while/body/eval_jaxpr/ppermute | solution.py:12
  85.2 7.6 %collective-permute-done.1 = bf16[128,256]{1,0:T(8,128)(2,1)S(1)} collective-permute-done((bf16[128,256]{1,0:T(8,128)(2,1)S(1)}, bf16[128,256]{1,0:T(8,128)(2,1)S(1)}, u32[]{:S(2)}, u32[]{:S(2)}) %collective-permute-start.1) | collective-permute-done | bytes 65568 | tf_op jit(solution)/shard_map/while/body/eval_jaxpr/ppermute | solution.py:12
  92.8 1.9 %collective-permute-start.1 = (bf16[128,256]{1,0:T(8,128)(2,1)S(1)}, bf16[128,256]{1,0:T(8,128)(2,1)S(1)}, u32[]{:S(2)}, u32[]{:S(2)}) collective-permute-start(bf16[128,256]{1,0:T(8,128)(2,1)S(1)} %get-tuple-element.898), channel_id=1, source_target_pairs={{8,0},{16,8},{24,16},{32,24},{40,32},{48,40},{56,48},{64,56},{72,6... | collective-permute-start | bytes 196616 | tf_op jit(solution)/shard_map/while/body/eval_jaxpr/ppermute | solution.py:12
  94.8 7.0 %collective-permute-done.1 = bf16[128,256]{1,0:T(8,128)(2,1)S(1)} collective-permute-done((bf16[128,256]{1,0:T(8,128)(2,1)S(1)}, bf16[128,256]{1,0:T(8,128)(2,1)S(1)}, u32[]{:S(2)}, u32[]{:S(2)}) %collective-permute-start.1) | collective-permute-done | bytes 65568 | tf_op jit(solution)/shard_map/while/body/eval_jaxpr/ppermute | solution.py:12
  101.8 1.9 %collective-permute-start.1 = (bf16[128,256]{1,0:T(8,128)(2,1)S(1)}, bf16[128,256]{1,0:T(8,128)(2,1)S(1)}, u32[]{:S(2)}, u32[]{:S(2)}) collective-permute-start(bf16[128,256]{1,0:T(8,128)(2,1)S(1)} %get-tuple-element.898), channel_id=1, source_target_pairs={{8,0},{16,8},{24,16},{32,24},{40,32},{48,40},{56,48},{64,56},{72,6... | collective-permute-start | bytes 196616 | tf_op jit(solution)/shard_map/while/body/eval_jaxpr/ppermute | solution.py:12
  103.7 7.0 %collective-permute-done.1 = bf16[128,256]{1,0:T(8,128)(2,1)S(1)} collective-permute-done((bf16[128,256]{1,0:T(8,128)(2,1)S(1)}, bf16[128,256]{1,0:T(8,128)(2,1)S(1)}, u32[]{:S(2)}, u32[]{:S(2)}) %collective-permute-start.1) | collective-permute-done | bytes 65568 | tf_op jit(solution)/shard_map/while/body/eval_jaxpr/ppermute | solution.py:12
  110.7 1.9 %collective-permute-start.1 = (bf16[128,256]{1,0:T(8,128)(2,1)S(1)}, bf16[128,256]{1,0:T(8,128)(2,1)S(1)}, u32[]{:S(2)}, u32[]{:S(2)}) collective-permute-start(bf16[128,256]{1,0:T(8,128)(2,1)S(1)} %get-tuple-element.898), channel_id=1, source_target_pairs={{8,0},{16,8},{24,16},{32,24},{40,32},{48,40},{56,48},{64,56},{72,6... | collective-permute-start | bytes 196616 | tf_op jit(solution)/shard_map/while/body/eval_jaxpr/ppermute | solution.py:12
  112.6 7.0 %collective-permute-done.1 = bf16[128,256]{1,0:T(8,128)(2,1)S(1)} collective-permute-done((bf16[128,256]{1,0:T(8,128)(2,1)S(1)}, bf16[128,256]{1,0:T(8,128)(2,1)S(1)}, u32[]{:S(2)}, u32[]{:S(2)}) %collective-permute-start.1) | collective-permute-done | bytes 65568 | tf_op jit(solution)/shard_map/while/body/eval_jaxpr/ppermute | solution.py:12
  119.6 1.9 %collective-permute-start.1 = (bf16[128,256]{1,0:T(8,128)(2,1)S(1)}, bf16[128,256]{1,0:T(8,128)(2,1)S(1)}, u32[]{:S(2)}, u32[]{:S(2)}) collective-permute-start(bf16[128,256]{1,0:T(8,128)(2,1)S(1)} %get-tuple-element.898), channel_id=1, source_target_pairs={{8,0},{16,8},{24,16},{32,24},{40,32},{48,40},{56,48},{64,56},{72,6... | collective-permute-start | bytes 196616 | tf_op jit(solution)/shard_map/while/body/eval_jaxpr/ppermute | solution.py:12
  121.6 7.0 %collective-permute-done.1 = bf16[128,256]{1,0:T(8,128)(2,1)S(1)} collective-permute-done((bf16[128,256]{1,0:T(8,128)(2,1)S(1)}, bf16[128,256]{1,0:T(8,128)(2,1)S(1)}, u32[]{:S(2)}, u32[]{:S(2)}) %collective-permute-start.1) | collective-permute-done | bytes 65568 | tf_op jit(solution)/shard_map/while/body/eval_jaxpr/ppermute | solution.py:12
  128.6 1.9 %collective-permute-start.1 = (bf16[128,256]{1,0:T(8,128)(2,1)S(1)}, bf16[128,256]{1,0:T(8,128)(2,1)S(1)}, u32[]{:S(2)}, u32[]{:S(2)}) collective-permute-start(bf16[128,256]{1,0:T(8,128)(2,1)S(1)} %get-tuple-element.898), channel_id=1, source_target_pairs={{8,0},{16,8},{24,16},{32,24},{40,32},{48,40},{56,48},{64,56},{72,6... | collective-permute-start | bytes 196616 | tf_op jit(solution)/shard_map/while/body/eval_jaxpr/ppermute | solution.py:12
  130.5 7.0 %collective-permute-done.1 = bf16[128,256]{1,0:T(8,128)(2,1)S(1)} collective-permute-done((bf16[128,256]{1,0:T(8,128)(2,1)S(1)}, bf16[128,256]{1,0:T(8,128)(2,1)S(1)}, u32[]{:S(2)}, u32[]{:S(2)}) %collective-permute-start.1) | collective-permute-done | bytes 65568 | tf_op jit(solution)/shard_map/while/body/eval_jaxpr/ppermute | solution.py:12
  137.5 1.9 %collective-permute-start.1 = (bf16[128,256]{1,0:T(8,128)(2,1)S(1)}, bf16[128,256]{1,0:T(8,128)(2,1)S(1)}, u32[]{:S(2)}, u32[]{:S(2)}) collective-permute-start(bf16[128,256]{1,0:T(8,128)(2,1)S(1)} %get-tuple-element.898), channel_id=1, source_target_pairs={{8,0},{16,8},{24,16},{32,24},{40,32},{48,40},{56,48},{64,56},{72,6... | collective-permute-start | bytes 196616 | tf_op jit(solution)/shard_map/while/body/eval_jaxpr/ppermute | solution.py:12
  139.5 7.0 %collective-permute-done.1 = bf16[128,256]{1,0:T(8,128)(2,1)S(1)} collective-permute-done((bf16[128,256]{1,0:T(8,128)(2,1)S(1)}, bf16[128,256]{1,0:T(8,128)(2,1)S(1)}, u32[]{:S(2)}, u32[]{:S(2)}) %collective-permute-start.1) | collective-permute-done | bytes 65568 | tf_op jit(solution)/shard_map/while/body/eval_jaxpr/ppermute | solution.py:12
  (169 shorter events, 26.3 us)
Async XLA Ops:
  0.6 2.9 %copy-start = (bf16[128,1024]{1,0:T(8,128)(2,1)S(1)}, bf16[128,1024]{1,0:T(8,128)(2,1)}, u32[]{:S(2)}) copy-start(bf16[128,1024]{1,0:T(8,128)(2,1)} %param.17) | copy-start | bytes 786436
  3.5 1.0 copy-start.1
  4.7 4.6 %collective-permute-start = (bf16[128,256]{1,0:T(8,128)(2,1)S(1)}, bf16[128,256]{1,0:T(8,128)(2,1)S(1)}, u32[]{:S(2)}, u32[]{:S(2)}) collective-permute-start(bf16[128,256]{1,0:T(8,128)(2,1)S(1)} %get-tuple-element.771), channel_id=1, source_target_pairs={{0,8},{8,16},{16,24},{24,32},{32,40},{40,48},{48,56},{56,64},{64,7... | collective-permute-start | bytes 196616 | tf_op jit(solution)/shard_map/while/body/eval_jaxpr/ppermute | solution.py:12
  9.3 8.9 %collective-permute-start = (bf16[128,256]{1,0:T(8,128)(2,1)S(1)}, bf16[128,256]{1,0:T(8,128)(2,1)S(1)}, u32[]{:S(2)}, u32[]{:S(2)}) collective-permute-start(bf16[128,256]{1,0:T(8,128)(2,1)S(1)} %get-tuple-element.771), channel_id=1, source_target_pairs={{0,8},{8,16},{16,24},{24,32},{32,40},{40,48},{48,56},{56,64},{64,7... | collective-permute-start | bytes 196616 | tf_op jit(solution)/shard_map/while/body/eval_jaxpr/ppermute | solution.py:12
  18.2 8.9 %collective-permute-start = (bf16[128,256]{1,0:T(8,128)(2,1)S(1)}, bf16[128,256]{1,0:T(8,128)(2,1)S(1)}, u32[]{:S(2)}, u32[]{:S(2)}) collective-permute-start(bf16[128,256]{1,0:T(8,128)(2,1)S(1)} %get-tuple-element.771), channel_id=1, source_target_pairs={{0,8},{8,16},{16,24},{24,32},{32,40},{40,48},{48,56},{56,64},{64,7... | collective-permute-start | bytes 196616 | tf_op jit(solution)/shard_map/while/body/eval_jaxpr/ppermute | solution.py:12
  27.2 8.9 %collective-permute-start = (bf16[128,256]{1,0:T(8,128)(2,1)S(1)}, bf16[128,256]{1,0:T(8,128)(2,1)S(1)}, u32[]{:S(2)}, u32[]{:S(2)}) collective-permute-start(bf16[128,256]{1,0:T(8,128)(2,1)S(1)} %get-tuple-element.771), channel_id=1, source_target_pairs={{0,8},{8,16},{16,24},{24,32},{32,40},{40,48},{48,56},{56,64},{64,7... | collective-permute-start | bytes 196616 | tf_op jit(solution)/shard_map/while/body/eval_jaxpr/ppermute | solution.py:12
  36.1 8.9 %collective-permute-start = (bf16[128,256]{1,0:T(8,128)(2,1)S(1)}, bf16[128,256]{1,0:T(8,128)(2,1)S(1)}, u32[]{:S(2)}, u32[]{:S(2)}) collective-permute-start(bf16[128,256]{1,0:T(8,128)(2,1)S(1)} %get-tuple-element.771), channel_id=1, source_target_pairs={{0,8},{8,16},{16,24},{24,32},{32,40},{40,48},{48,56},{56,64},{64,7... | collective-permute-start | bytes 196616 | tf_op jit(solution)/shard_map/while/body/eval_jaxpr/ppermute | solution.py:12
  45.0 8.9 %collective-permute-start = (bf16[128,256]{1,0:T(8,128)(2,1)S(1)}, bf16[128,256]{1,0:T(8,128)(2,1)S(1)}, u32[]{:S(2)}, u32[]{:S(2)}) collective-permute-start(bf16[128,256]{1,0:T(8,128)(2,1)S(1)} %get-tuple-element.771), channel_id=1, source_target_pairs={{0,8},{8,16},{16,24},{24,32},{32,40},{40,48},{48,56},{56,64},{64,7... | collective-permute-start | bytes 196616 | tf_op jit(solution)/shard_map/while/body/eval_jaxpr/ppermute | solution.py:12
  54.0 8.9 %collective-permute-start = (bf16[128,256]{1,0:T(8,128)(2,1)S(1)}, bf16[128,256]{1,0:T(8,128)(2,1)S(1)}, u32[]{:S(2)}, u32[]{:S(2)}) collective-permute-start(bf16[128,256]{1,0:T(8,128)(2,1)S(1)} %get-tuple-element.771), channel_id=1, source_target_pairs={{0,8},{8,16},{16,24},{24,32},{32,40},{40,48},{48,56},{56,64},{64,7... | collective-permute-start | bytes 196616 | tf_op jit(solution)/shard_map/while/body/eval_jaxpr/ppermute | solution.py:12
  83.3 9.5 %collective-permute-start.1 = (bf16[128,256]{1,0:T(8,128)(2,1)S(1)}, bf16[128,256]{1,0:T(8,128)(2,1)S(1)}, u32[]{:S(2)}, u32[]{:S(2)}) collective-permute-start(bf16[128,256]{1,0:T(8,128)(2,1)S(1)} %get-tuple-element.898), channel_id=1, source_target_pairs={{8,0},{16,8},{24,16},{32,24},{40,32},{48,40},{56,48},{64,56},{72,6... | collective-permute-start | bytes 196616 | tf_op jit(solution)/shard_map/while/body/eval_jaxpr/ppermute | solution.py:12
  92.8 8.9 %collective-permute-start.1 = (bf16[128,256]{1,0:T(8,128)(2,1)S(1)}, bf16[128,256]{1,0:T(8,128)(2,1)S(1)}, u32[]{:S(2)}, u32[]{:S(2)}) collective-permute-start(bf16[128,256]{1,0:T(8,128)(2,1)S(1)} %get-tuple-element.898), channel_id=1, source_target_pairs={{8,0},{16,8},{24,16},{32,24},{40,32},{48,40},{56,48},{64,56},{72,6... | collective-permute-start | bytes 196616 | tf_op jit(solution)/shard_map/while/body/eval_jaxpr/ppermute | solution.py:12
  101.8 8.9 %collective-permute-start.1 = (bf16[128,256]{1,0:T(8,128)(2,1)S(1)}, bf16[128,256]{1,0:T(8,128)(2,1)S(1)}, u32[]{:S(2)}, u32[]{:S(2)}) collective-permute-start(bf16[128,256]{1,0:T(8,128)(2,1)S(1)} %get-tuple-element.898), channel_id=1, source_target_pairs={{8,0},{16,8},{24,16},{32,24},{40,32},{48,40},{56,48},{64,56},{72,6... | collective-permute-start | bytes 196616 | tf_op jit(solution)/shard_map/while/body/eval_jaxpr/ppermute | solution.py:12
  110.7 8.9 %collective-permute-start.1 = (bf16[128,256]{1,0:T(8,128)(2,1)S(1)}, bf16[128,256]{1,0:T(8,128)(2,1)S(1)}, u32[]{:S(2)}, u32[]{:S(2)}) collective-permute-start(bf16[128,256]{1,0:T(8,128)(2,1)S(1)} %get-tuple-element.898), channel_id=1, source_target_pairs={{8,0},{16,8},{24,16},{32,24},{40,32},{48,40},{56,48},{64,56},{72,6... | collective-permute-start | bytes 196616 | tf_op jit(solution)/shard_map/while/body/eval_jaxpr/ppermute | solution.py:12
  119.6 8.9 %collective-permute-start.1 = (bf16[128,256]{1,0:T(8,128)(2,1)S(1)}, bf16[128,256]{1,0:T(8,128)(2,1)S(1)}, u32[]{:S(2)}, u32[]{:S(2)}) collective-permute-start(bf16[128,256]{1,0:T(8,128)(2,1)S(1)} %get-tuple-element.898), channel_id=1, source_target_pairs={{8,0},{16,8},{24,16},{32,24},{40,32},{48,40},{56,48},{64,56},{72,6... | collective-permute-start | bytes 196616 | tf_op jit(solution)/shard_map/while/body/eval_jaxpr/ppermute | solution.py:12
  128.6 8.9 %collective-permute-start.1 = (bf16[128,256]{1,0:T(8,128)(2,1)S(1)}, bf16[128,256]{1,0:T(8,128)(2,1)S(1)}, u32[]{:S(2)}, u32[]{:S(2)}) collective-permute-start(bf16[128,256]{1,0:T(8,128)(2,1)S(1)} %get-tuple-element.898), channel_id=1, source_target_pairs={{8,0},{16,8},{24,16},{32,24},{40,32},{48,40},{56,48},{64,56},{72,6... | collective-permute-start | bytes 196616 | tf_op jit(solution)/shard_map/while/body/eval_jaxpr/ppermute | solution.py:12
  137.5 8.9 %collective-permute-start.1 = (bf16[128,256]{1,0:T(8,128)(2,1)S(1)}, bf16[128,256]{1,0:T(8,128)(2,1)S(1)}, u32[]{:S(2)}, u32[]{:S(2)}) collective-permute-start(bf16[128,256]{1,0:T(8,128)(2,1)S(1)} %get-tuple-element.898), channel_id=1, source_target_pairs={{8,0},{16,8},{24,16},{32,24},{40,32},{48,40},{56,48},{64,56},{72,6... | collective-permute-start | bytes 196616 | tf_op jit(solution)/shard_map/while/body/eval_jaxpr/ppermute | solution.py:12
where the time goes:
time: 149 us; the launch traced here: 148 us
  starting transfers between devices  62.3 us (42%)
  waiting for transfers between devices  58.5 us (39%)
  matrix products  13.1 us (9%)
  local copies, waits for them, and re-layouts  8.9 us (6%)
  other arithmetic  3.06 us (2%)
    ppermute x14, starting transfers between devices, shifted(): lax.ppermute(value, axis, [(source, source + steps) for source in range(f...  62.3 us
    ppermute x14, waiting for transfers between devices, shifted(): lax.ppermute(value, axis, [(source, source + steps) for source in range(f...  58.5 us
    dot_general x8, matrix products, tile_scores(): lax.dot_general(rows_query, key_tile, contract_last, preferred_element_ty...  4.1 us
    dot_general x4, matrix products, output_step(): jnp.dot(weights_bf, kv_tile[:, head_width:], preferred_element_type=jnp.f...  3.43 us
  transfers between devices with their start and end apart: 14, of which 14 were waited for; matrix products, arithmetic and copies ran while one was open for 0% of the time, Pallas kernels for 0%

commit v1 on v0

v1 whole, which is shorter than its diff:
```python
import functools
import math

import jax
import jax.numpy as jnp
from jax import lax
from jax.experimental import pallas as pl
from jax.experimental.pallas import tpu as pltpu
from jax.sharding import PartitionSpec as P

MESH = pl.DeviceIdType.MESH
HIDDEN = -1e30
CHUNK = 256
EARLY = (0, 2, 1, 4, 3)
LATE = (6, 5, 7)
BACK = (7, 5, 3, 1, 6, 4, 2, 0)


def dot(left, right):
    return jnp.dot(left, right, preferred_element_type=jnp.float32)


def kernel(
    q_hbm, k_hbm, v_hbm, g_hbm, docs_hbm, att_hbm, dq_hbm, dk_hbm, dv_hbm,
    kbuf, vbuf, q_rows, g_rows, q_t, g_t, k_t, v_t, s_ref, dp_ref, p_bf, ds_bf, o_t,
    att, dq, part_v, part_k, send_v, send_k, mate_v, mate_k, far_v, far_k, out_k, out_v, docs,
    load_sem, store_sem, ks_sem, kr_sem, vs_sem, vr_sem, gs_sem, gr_sem, hs_sem, hr_sem,
):
    me, head = lax.axis_index("seq"), lax.axis_index("head")
    count = lax.axis_size("seq")
    odd = lax.rem(me, 2)
    mate = me + 1 - 2 * odd
    cross = lax.rem(me - 3 + 6 * odd + count, count)
    rows, width = k_hbm.shape
    heads = q_hbm.shape[1] // width
    total = rows * heads
    chunks = [slice(at, at + CHUNK) for at in range(0, total, CHUNK)]

    def away(steps):
        return lax.rem(me + steps + count, count)

    def remote(src, dst, send_sem, recv_sem, device):
        return pltpu.make_async_remote_copy(
            src_ref=src, dst_ref=dst, send_sem=send_sem, recv_sem=recv_sem,
            device_id=(device, head), device_id_type=MESH,
        )

    barrier = pltpu.get_barrier_semaphore()
    peers = [away(-4), away(4), cross, away(-2), away(2), mate]
    for peer in peers:
        pl.semaphore_signal(barrier, inc=1, device_id=(peer, head), device_id_type=MESH)

    def load(src, dst, at):
        copy = pltpu.make_async_copy(src, dst, load_sem.at[at])
        copy.start()
        return copy

    load_k = load(k_hbm, kbuf.at[0], 0)
    load_v = load(v_hbm, vbuf.at[0], 1)
    load_docs = load(docs_hbm, docs, 2)
    spans = [pl.ds(h * width, width) for h in range(heads)]
    tiles = [pl.ds(h * rows, rows) for h in range(heads)]
    load_q = [load(q_hbm.at[:, spans[h]], q_rows.at[tiles[h]], 3 + h) for h in range(heads)]
    load_g = [load(g_hbm.at[:, spans[h]], g_rows.at[tiles[h]], 3 + heads + h) for h in range(heads)]
    load_k.wait()
    load_v.wait()
    pl.semaphore_wait(barrier, len(peers))

    class Forward:
        def __init__(self, buf, send_sem, recv_sem):
            self.buf, self.send_sem, self.recv_sem, self.sent = buf, send_sem, recv_sem, []

        def push(self, slot, to_slot, device, at):
            copy = remote(
                self.buf.at[slot], self.buf.at[to_slot], self.send_sem.at[at],
                self.recv_sem.at[to_slot], device,
            )
            copy.start()
            return copy

        def wait(self, slot):
            remote(
                self.buf.at[slot], self.buf.at[slot], self.send_sem.at[0], self.recv_sem.at[slot], mate
            ).wait_recv()

        def own(self):
            self.sent.append(self.push(0, 4, away(4), 0))
            self.sent.append(self.push(0, 2, away(2), 1))

            @pl.when(odd == 0)
            def _():
                self.push(0, 1, mate, 6)

        def to_mate(self, slot, at):
            self.sent.append(self.push(slot, slot + 1 - 2 * odd, mate, at))

        def got2(self):
            self.wait(2)
            self.to_mate(2, 2)

        def got4(self):
            self.wait(4)
            self.sent.append(self.push(4, 6, away(2), 3))

            @pl.when(odd == 1)
            def _():
                self.push(4, 7, cross, 6)

            self.to_mate(4, 4)

        def got6(self):
            self.wait(6)
            self.to_mate(6, 5)

        def finish(self):
            for copy in self.sent:
                copy.wait_send()
            remote(
                self.buf.at[0], self.buf.at[1], self.send_sem.at[6], self.recv_sem.at[1], mate
            ).wait_send()

    class Back:
        def __init__(self, part, send, mates, far, send_sem, recv_sem, out):
            self.part, self.send, self.mates, self.far = part, send, mates, far
            self.send_sem, self.recv_sem, self.out, self.sent = send_sem, recv_sem, out, []

        def push(self, slot, dst, recv_at, device):
            copy = remote(
                self.send.at[slot], dst, self.send_sem.at[slot], self.recv_sem.at[recv_at], device
            )
            copy.start()
            self.sent.append(copy)

        def wait(self, dst, recv_at):
            remote(
                self.send.at[0], dst, self.send_sem.at[0], self.recv_sem.at[recv_at], mate
            ).wait_recv()

        def wait_mate(self, slot):
            self.wait(self.mates.at[slot], slot)
            return self.mates[slot].astype(jnp.float32)

        def wait_far(self, slot):
            self.wait(self.far.at[slot], 9 + slot)
            return self.far[slot].astype(jnp.float32)

        def give(self, d, value):
            if d % 2 == 0:
                self.part[d] = value
                return
            self.send[d] = value.astype(jnp.bfloat16)
            device = jnp.where(odd == 0, cross, mate) if d == 7 else mate
            slot = d + 1 - 2 * odd
            self.push(d, self.mates.at[slot], slot, device)

        def relay6(self):
            self.send[6] = (self.part[6] + self.wait_mate(6)).astype(jnp.bfloat16)
            self.push(6, self.far.at[0], 9, away(-2))

        def relay2(self):
            self.send[2] = (self.part[2] + self.wait_mate(2)).astype(jnp.bfloat16)
            self.push(2, self.far.at[2], 11, away(-2))

        def relay4(self):
            self.part[4] = self.part[4] + self.wait_mate(4) + self.wait_far(0)

            @pl.when(odd == 1)
            def _():
                self.part[4] = self.part[4] + self.wait_mate(8)

            self.send[4] = self.part[4].astype(jnp.bfloat16)
            self.push(4, self.far.at[1], 10, away(-4))

        def final(self):
            self.part[0] = self.part[0] + self.wait_far(2) + self.wait_far(1)

            @pl.when(odd == 0)
            def _():
                self.part[0] = self.part[0] + self.wait_mate(0)

            self.out[...] = self.part[0].astype(jnp.bfloat16)

        def finish(self):
            for copy in self.sent:
                copy.wait_send()

    keys = Forward(kbuf, ks_sem, kr_sem)
    values = Forward(vbuf, vs_sem, vr_sem)
    back_v = Back(part_v, send_v, mate_v, far_v, gs_sem, gr_sem, out_v)
    back_k = Back(part_k, send_k, mate_k, far_k, hs_sem, hr_sem, out_k)
    keys.own()
    values.own()

    load_docs.wait()
    end, start = jnp.int32(0), jnp.int32(0)
    for at in range(docs.shape[0]):
        end = end + docs[at]
        start = jnp.where(end <= me, end, start)
    reach = me - start
    hidden = [jnp.where(d <= reach, 0.0, HIDDEN).astype(jnp.float32) for d in range(8)]

    for h in range(heads):
        load_q[h].wait()
        q_t[:, spans[h]] = q_rows[tiles[h]].T

    score_scale = width ** (-0.5)
    rate = score_scale * math.log2(math.e)
    causal = lax.broadcasted_iota(jnp.int32, (rows, CHUNK), 0) <= (
        lax.broadcasted_iota(jnp.int32, (rows, CHUNK), 1) % rows
    )

    def score(d, tops):
        out = []
        for at, cols in enumerate(chunks):
            scores = dot(kbuf[d], q_t[:, cols])
            if d == 0:
                scores = jnp.where(causal, scores, HIDDEN)
            s_ref[d, :, cols] = scores
            top = jnp.max(scores, axis=0, keepdims=True) + hidden[d]
            out.append(top if tops is None else jnp.maximum(tops[at], top))
        k_t[:, d * rows : (d + 1) * rows] = kbuf[d].T
        return out

    def lift(d, tops, sums):
        out = []
        for at, cols in enumerate(chunks):
            raised = jnp.exp2(s_ref[d, :, cols] * rate - (tops[at] * rate - hidden[d]))
            s_ref[d, :, cols] = raised
            part = jnp.sum(raised, axis=0, keepdims=True)
            out.append(part if sums is None else sums[at] + part)
        return out

    tops = score(0, None)
    for h in range(heads):
        load_g[h].wait()
        g_t[:, spans[h]] = g_rows[tiles[h]].T
    v_t[:, 0:rows] = vbuf[0].T

    keys.got2()
    keys.got4()
    tops = score(2, tops)
    tops = score(4, tops)
    values.got2()
    keys.wait(1)
    tops = score(1, tops)
    keys.wait(3)
    tops = score(3, tops)
    values.got4()
    sums = None
    for d in EARLY:
        sums = lift(d, tops, sums)
    keys.got6()
    late = score(6, tops)
    keys.wait(7)
    late = score(7, late)
    keys.wait(5)
    late = score(5, late)
    late_sums = None
    for d in LATE:
        late_sums = lift(d, late, late_sums)
    early_norm, late_norm = [], []
    for at in range(len(chunks)):
        fade = jnp.exp2((tops[at] - late[at]) * rate)
        norm = 1.0 / (sums[at] * fade + late_sums[at])
        early_norm.append(fade * norm)
        late_norm.append(norm)

    for d in BACK:
        for at, cols in enumerate(chunks):
            norm = late_norm[at] if d in LATE else early_norm[at]
            weights = s_ref[d, :, cols] * norm
            s_ref[d, :, cols] = weights
            p_bf[d * rows : (d + 1) * rows, cols] = weights.astype(jnp.bfloat16)
        back_v.give(d, dot(p_bf[d * rows : (d + 1) * rows, :], g_rows[...]))

    def value_tile(d):
        v_t[:, d * rows : (d + 1) * rows] = vbuf[d].T
        for cols in chunks:
            dp_ref[d, :, cols] = dot(vbuf[d], g_t[:, cols])

    values.got6()
    for d in (0, 2, 4, 6):
        value_tile(d)
    back_v.relay6()
    for d in (1, 3, 7):
        values.wait(d)
        value_tile(d)
    back_v.relay2()
    values.wait(5)
    value_tile(5)
    back_v.relay4()

    deltas = []
    for cols in chunks:
        rounded = dot(v_t[...], p_bf[:, cols]).astype(jnp.bfloat16).astype(jnp.float32)
        o_t[:, cols] = rounded
        deltas.append(jnp.sum(rounded * g_t[:, cols].astype(jnp.float32), axis=0, keepdims=True))

    for d in BACK:
        for at, cols in enumerate(chunks):
            change = s_ref[d, :, cols] * (dp_ref[d, :, cols] - deltas[at]) * score_scale
            ds_bf[d * rows : (d + 1) * rows, cols] = change.astype(jnp.bfloat16)
        back_k.give(d, dot(ds_bf[d * rows : (d + 1) * rows, :], q_rows[...]))

    def store(src, dst, at):
        copy = pltpu.make_async_copy(src, dst, store_sem.at[at])
        copy.start()
        return copy

    for h in range(heads):
        att[:, spans[h]] = o_t[:, h * rows : (h + 1) * rows].T.astype(jnp.bfloat16)
    stores = [store(att, att_hbm, 0)]
    back_k.relay6()
    back_k.relay2()
    for cols in chunks:
        grads = dot(k_t[...], ds_bf[:, cols])
        for at in range(CHUNK // rows):
            h = cols.start // rows + at
            dq[:, spans[h]] = grads[:, at * rows : (at + 1) * rows].T.astype(jnp.bfloat16)
    stores.append(store(dq, dq_hbm, 1))
    back_k.relay4()
    back_v.final()
    stores.append(store(out_v, dv_hbm, 2))
    back_k.final()
    stores.append(store(out_k, dk_hbm, 3))
    for part in (keys, values, back_v, back_k):
        part.finish()
    for copy in stores:
        copy.wait()


def local(queries, key_rows, value_rows, out_grad, doc_blocks):
    rows, width = key_rows.shape
    heads = queries.shape[1] // width
    total = rows * heads
    span = 8 * rows
    bf, f32 = jnp.bfloat16, jnp.float32
    blocks = pltpu.VMEM((8, rows, width), bf)
    dma = pltpu.SemaphoreType.DMA
    anywhere = pl.BlockSpec(memory_space=pl.ANY)
    scratch = [
        blocks, blocks,
        pltpu.VMEM((total, width), bf), pltpu.VMEM((total, width), bf),
        pltpu.VMEM((width, total), bf), pltpu.VMEM((width, total), bf),
        pltpu.VMEM((width, span), bf), pltpu.VMEM((width, span), bf),
        pltpu.VMEM((8, rows, total), f32), pltpu.VMEM((8, rows, total), f32),
        pltpu.VMEM((span, total), bf), pltpu.VMEM((span, total), bf),
        pltpu.VMEM((width, total), f32),
        pltpu.VMEM((rows, heads * width), bf), pltpu.VMEM((rows, heads * width), bf),
        pltpu.VMEM((8, rows, width), f32), pltpu.VMEM((8, rows, width), f32),
        blocks, blocks,
        pltpu.VMEM((9, rows, width), bf), pltpu.VMEM((9, rows, width), bf),
        pltpu.VMEM((3, rows, width), bf), pltpu.VMEM((3, rows, width), bf),
        pltpu.VMEM((rows, width), bf), pltpu.VMEM((rows, width), bf),
        pltpu.SMEM(doc_blocks.shape, jnp.int32),
        dma((3 + 2 * heads,)), dma((4,)),
        dma((7,)), dma((8,)), dma((7,)), dma((8,)),
        dma((8,)), dma((12,)), dma((8,)), dma((12,)),
    ]
    return pl.pallas_call(
        kernel,
        out_shape=(
            jax.ShapeDtypeStruct(queries.shape, bf),
            jax.ShapeDtypeStruct(queries.shape, bf),
            jax.ShapeDtypeStruct(key_rows.shape, bf),
            jax.ShapeDtypeStruct(key_rows.shape, bf),
        ),
        in_specs=[anywhere] * 5,
        out_specs=(anywhere,) * 4,
        scratch_shapes=scratch,
        name="packed_attention",
        compiler_params=pltpu.CompilerParams(collective_id=0, has_side_effects=True),
    )(queries, key_rows, value_rows, out_grad, doc_blocks)


def solution(mesh):
    in_specs = (P("seq", "head"), P("seq", "head"), P("seq", "head"), P("seq", "head"), P())
    out_specs = (P("seq", "head"), P("seq", "head"), P("seq", "head"), P("seq", "head"))
    return jax.shard_map(local, mesh=mesh, in_specs=in_specs, out_specs=out_specs, check_vma=False)
```

time: 149 us -> 44.5 us (0.30)
  the two profiles are of different devices: /device:TPU:503 before, /device:TPU:94 now
where the time goes in v1:
time: 44.5 us; the launch traced here: 44.1 us
  Pallas kernels  39.6 us (89%)
  local copies, waits for them, and re-layouts  3.86 us (9%)
  between operations  0.65 us (1%)
    pallas_call x1, Pallas kernels, local(): pl.pallas_call(kernel, out_shape=(jax.ShapeDtypeStruct(queries.shape, bf)...  39.6 us
    unnamed x10, local copies, waits for them, and re-layouts  3.86 us

profile of v1, /device:TPU:94, one launch (start us, length us, event | category | flops | bytes accessed | tf_op | source)
XLA Modules:
  0.0 44.1 jit_solution(714228220303615487)
XLA Ops:
  0.6 39.6 %packed_attention.1 = (bf16[128,1024]{1,0:T(8,128)(2,1)}, bf16[128,1024]{1,0:T(8,128)(2,1)}, bf16[128,128]{1,0:T(8,128)(2,1)}, bf16[128,128]{1,0:T(8,128)(2,1)}) custom-call(bf16[128,1024]{1,0:T(8,128)(2,1)} %q_hbm.1, bf16[128,128]{1,0:T(8,128)(2,1)} %k_hbm.1, bf16[128,128]{1,0:T(8,128)(2,1)} %v_hbm.1, bf16[128,1024]{1,0:T(8,128)(2,1)} %g_hbm.1, s32[64]{0:T(128)} %docs_hbm.1), custom_call_target="tpu_custom_call" | custom-call | tf_op jit(solution)/shard_map/packed_attention/pallas_call | solution.py:360
  40.3 0.0 copy-start
  40.3 1.7 %copy.13 = bf16[128,1024]{1,0:T(8,128)(2,1)} copy(bf16[128,1024]{1,0:T(8,128)(2,1)} %get-tuple-element.8) | data formatting | bytes 524288
  42.0 0.0 copy-done
  42.0 0.0 copy-start.2
  42.0 0.7 %copy.14 = bf16[128,1024]{1,0:T(8,128)(2,1)} copy(bf16[128,1024]{1,0:T(8,128)(2,1)S(1)} %copy-done) | data formatting | bytes 524288
  42.7 0.1 copy-done.2
  42.7 0.0 copy-start.1
  42.8 0.6 %copy.15 = bf16[128,128]{1,0:T(8,128)(2,1)} copy(bf16[128,128]{1,0:T(8,128)(2,1)S(1)} %copy-done.2) | data formatting | bytes 65536
  43.4 0.2 copy-done.1
  43.5 0.6 %copy.16 = bf16[128,128]{1,0:T(8,128)(2,1)} copy(bf16[128,128]{1,0:T(8,128)(2,1)S(1)} %copy-done.1) | data formatting | bytes 65536
Async XLA Ops:
  40.3 1.7 %copy-start = (bf16[128,1024]{1,0:T(8,128)(2,1)S(1)}, bf16[128,1024]{1,0:T(8,128)(2,1)}, u32[]{:S(2)}) copy-start(bf16[128,1024]{1,0:T(8,128)(2,1)} %get-tuple-element.9) | copy-start | bytes 786436
  42.0 0.8 %copy-start.2 = (bf16[128,128]{1,0:T(8,128)(2,1)S(1)}, bf16[128,128]{1,0:T(8,128)(2,1)}, u32[]{:S(2)}) copy-start(bf16[128,128]{1,0:T(8,128)(2,1)} %get-tuple-element.10) | copy-start | bytes 98308
  42.7 0.8 %copy-start.1 = (bf16[128,128]{1,0:T(8,128)(2,1)S(1)}, bf16[128,128]{1,0:T(8,128)(2,1)}, u32[]{:S(2)}) copy-start(bf16[128,128]{1,0:T(8,128)(2,1)} %get-tuple-element.11) | copy-start | bytes 98308

commit v2 on v1

v2 whole, which is shorter than its diff:
```python
import functools
import math

import jax
import jax.numpy as jnp
from jax import lax
from jax.experimental import pallas as pl
from jax.experimental.pallas import tpu as pltpu
from jax.sharding import PartitionSpec as P

MESH = pl.DeviceIdType.MESH
HIDDEN = -1e30
CHUNK = 256
SLOTS = 8
BACK = (7, 5, 3, 1, 6, 4, 2, 0)


def dot(left, right):
    return jnp.dot(left, right, preferred_element_type=jnp.float32)


def kernel(
    q_hbm, k_hbm, v_hbm, g_hbm, docs_hbm, att_out, dq_out, dk_out, dv_out,
    kbuf, vbuf, q_rows, g_rows, q_t, g_t, k_t, v_t, s_ref, dp_ref, p_bf, ds_bf, o_t,
    att, dq, part_v, part_k, send_v, send_k, mate_v, mate_k, far_v, far_k, out_k, out_v, docs,
    load_sem, store_sem, ks_sem, kr_sem, vs_sem, vr_sem, gs_sem, gm_sem, gf_sem, hs_sem, hm_sem, hf_sem,
):
    me, head = lax.axis_index("seq"), lax.axis_index("head")
    final_device = lax.axis_size("seq") - 1
    odd = lax.rem(me, 2)
    even = odd == 0
    mate = me + 1 - 2 * odd
    rows, width = k_hbm.shape
    heads = q_hbm.shape[1] // width
    total = rows * heads
    chunks = [slice(at, at + CHUNK) for at in range(0, total, CHUNK)]
    last = jnp.where((me >= 1) & (me < SLOTS), me, SLOTS - 1)

    def remote(src, dst, send_sem, recv_sem, device):
        return pltpu.make_async_remote_copy(
            src_ref=src, dst_ref=dst, send_sem=send_sem, recv_sem=recv_sem,
            device_id=(device, head), device_id_type=MESH,
        )

    barrier = pltpu.get_barrier_semaphore()

    def greet(when, device):
        @pl.when(when)
        def _():
            pl.semaphore_signal(barrier, inc=1, device_id=(device, head), device_id_type=MESH)

    greet(me >= 6, jnp.where(me < 8, 0, me - 4))
    greet((me >= 4) & (me < 8), me - 4)
    greet((me >= 8) & even, me - 3)
    greet(me >= 2, me - 2)
    greet((odd == 1) | (me >= 2), mate)

    def load(src, dst, at):
        copy = pltpu.make_async_copy(src, dst, load_sem.at[at])
        copy.start()
        return copy

    load_k = load(k_hbm, kbuf.at[0], 0)
    load_v = load(v_hbm, vbuf.at[0], 1)
    load_docs = load(docs_hbm, docs, 2)
    spans = [pl.ds(h * width, width) for h in range(heads)]
    tiles = [pl.ds(h * rows, rows) for h in range(heads)]
    load_q = [load(q_hbm.at[:, spans[h]], q_rows.at[tiles[h]], 3 + h) for h in range(heads)]
    load_g = [load(g_hbm.at[:, spans[h]], g_rows.at[tiles[h]], 3 + heads + h) for h in range(heads)]

    def yes(condition):
        return jnp.where(condition, 1, 0)

    pl.semaphore_wait(
        barrier,
        yes(me + 2 <= final_device) + yes(me + 4 <= final_device) + yes(even | (me >= 3))
        + yes((odd == 1) & (me >= 5) & (me + 3 <= final_device)) + 2 * yes(me == 0),
    )

    class Forward:
        def __init__(self, block, buf, send_sem, recv_sem):
            self.block, self.buf, self.send_sem, self.recv_sem = block, buf, send_sem, recv_sem
            self.sent = []

        def push(self, when, slot, to_slot, device, at):
            src = self.block if isinstance(slot, int) and slot == 0 else self.buf.at[slot]

            @pl.when(when)
            def _():
                remote(
                    src, self.buf.at[to_slot], self.send_sem.at[at], self.recv_sem.at[to_slot], device
                ).start()

            self.sent.append((when, at))

        def wait(self, slot, when=True):
            @pl.when((me >= slot) & when)
            def _():
                remote(
                    self.buf.at[slot], self.buf.at[slot], self.send_sem.at[0], self.recv_sem.at[slot], mate
                ).wait_recv()

        def far(self):
            self.push(me == 0, 0, 7, 7, 7)
            self.push(me == 0, 0, 6, 6, 8)

        def near(self):
            self.push(me + 4 <= final_device, 0, 4, me + 4, 0)
            self.push(even, 0, 1, mate, 6)
            self.push(me + 2 <= final_device, 0, 2, me + 2, 1)

        def across(self, slot, at, when):
            self.push((me >= slot) & when, slot, slot + 1 - 2 * odd, mate, at)

        def got(self, slot):
            ready = last != slot

            @pl.when(ready)
            def _():
                self.wait(slot)

            if slot == 4:
                self.push((me >= 5) & (me + 2 <= final_device), 4, 6, me + 2, 3)
                self.push((me >= 5) & (odd == 1) & (me + 3 <= final_device), 4, 7, me + 3, 9)
            self.across(slot, slot // 2 + 1 if slot < 6 else 5, ready)

        def got_last(self):
            self.wait(last)
            self.push((me == 2) | (me == 4), last, last + 1, mate, 10)

        def finish(self):
            for when, at in self.sent:
                @pl.when(when)
                def _():
                    remote(
                        self.buf.at[0], self.buf.at[1], self.send_sem.at[at], self.recv_sem.at[1], mate
                    ).wait_send()

    class Back:
        def __init__(self, part, send, mates, far, send_sem, mate_sem, far_sem, out):
            self.part, self.send, self.mates, self.far, self.out = part, send, mates, far, out
            self.send_sem, self.mate_sem, self.far_sem = send_sem, mate_sem, far_sem
            self.sent = []

        def push(self, when, d, dst, recv_sem, device):
            @pl.when(when)
            def _():
                remote(self.send.at[d], dst, self.send_sem.at[d], recv_sem, device).start()

        def give(self, d):
            slot = d + 1 - 2 * odd
            if d == 7:
                self.push((me >= d) & even, d, self.far.at[3], self.far_sem.at[3], me - d)
                self.push((me >= d) & (odd == 1), d, self.mates.at[6], self.mate_sem.at[6], mate)
            else:
                self.push(me >= d, d, self.mates.at[slot], self.mate_sem.at[slot], mate)
            self.sent.append(d)

        def wait_mate(self, slot):
            remote(
                self.send.at[0], self.mates.at[slot], self.send_sem.at[0], self.mate_sem.at[slot], mate
            ).wait_recv()
            return self.mates[slot].astype(jnp.float32)

        def wait_far(self, at):
            remote(
                self.send.at[0], self.far.at[at], self.send_sem.at[0], self.far_sem.at[at], mate
            ).wait_recv()
            return self.far[at].astype(jnp.float32)

        def relay(self, d):
            @pl.when(me >= d)
            def _():
                self.send[d] = (self.part[d] + self.wait_mate(d)).astype(jnp.bfloat16)
                at = d // 2 - 1
                remote(
                    self.send.at[d], self.far.at[at], self.send_sem.at[d], self.far_sem.at[at], me - d
                ).start()

            self.sent.append(d)

        def final(self):
            @pl.when(even)
            def _():
                self.part[0] = self.part[0] + self.wait_mate(0)

            for at, steps in ((0, 2), (1, 4), (2, 6)):
                @pl.when(me + steps <= final_device)
                def _():
                    self.part[0] = self.part[0] + self.wait_far(at)

            @pl.when((odd == 1) & (me + 7 <= final_device))
            def _():
                self.part[0] = self.part[0] + self.wait_far(3)

            self.out[...] = self.part[0].astype(jnp.bfloat16)

        def finish(self):
            for d in self.sent:
                @pl.when(me >= d)
                def _():
                    remote(
                        self.send.at[d], self.far.at[0], self.send_sem.at[d], self.far_sem.at[0], mate
                    ).wait_send()

    keys = Forward(k_hbm, kbuf, ks_sem, kr_sem)
    values = Forward(v_hbm, vbuf, vs_sem, vr_sem)
    back_v = Back(part_v, send_v, mate_v, far_v, gs_sem, gm_sem, gf_sem, out_v)
    back_k = Back(part_k, send_k, mate_k, far_k, hs_sem, hm_sem, hf_sem, out_k)
    keys.far()
    values.far()
    keys.near()
    values.near()

    for d in range(1, SLOTS):
        @pl.when(me < d)
        def _():
            kbuf[d] = jnp.zeros_like(kbuf[d])
            vbuf[d] = jnp.zeros_like(vbuf[d])

    load_docs.wait()
    end, start = jnp.int32(0), jnp.int32(0)
    for at in range(docs.shape[0]):
        end = end + docs[at]
        start = jnp.where(end <= me, end, start)
    reach = me - start

    def place(d):
        at = jnp.where(lax.rem(d, 2) == 1, (SLOTS - 1 - d) // 2, SLOTS - 1 - d // 2)
        return pl.ds(pl.multiple_of(at * rows, rows), rows)

    score_scale = width ** (-0.5)
    rate = score_scale * math.log2(math.e)
    causal = lax.broadcasted_iota(jnp.int32, (rows, CHUNK), 0) <= (
        lax.broadcasted_iota(jnp.int32, (rows, CHUNK), 1) % rows
    )

    def hidden(d):
        return jnp.where(d <= reach, 0.0, HIDDEN).astype(jnp.float32)

    def score(d, tops, own=False):
        out = []
        block = kbuf[d]
        for at, cols in enumerate(chunks):
            scores = dot(block, q_t[:, cols])
            if own:
                scores = jnp.where(causal, scores, HIDDEN)
            s_ref[d, :, cols] = scores
            top = jnp.max(scores, axis=0, keepdims=True) + hidden(d)
            out.append(top if tops is None else jnp.maximum(tops[at], top))
        k_t[:, place(d)] = block.T
        return out

    def lift(d, tops, sums):
        out = []
        for at, cols in enumerate(chunks):
            raised = jnp.exp2(s_ref[d, :, cols] * rate - (tops[at] * rate - hidden(d)))
            s_ref[d, :, cols] = raised
            part = jnp.sum(raised, axis=0, keepdims=True)
            out.append(part if sums is None else sums[at] + part)
        return out

    def value_tile(d):
        block = vbuf[d]
        v_t[:, place(d)] = block.T
        for cols in chunks:
            dp_ref[d, :, cols] = dot(block, g_t[:, cols])

    early = [jnp.int32(0)] + [j + yes(j >= last) for j in range(1, SLOTS - 1)]

    for h in range(heads):
        load_q[h].wait()
        q_t[:, spans[h]] = q_rows[tiles[h]].T
    keys.got(2)
    load_k.wait()
    tops = score(early[0], None, own=True)
    keys.got(4)
    values.got(2)
    for h in range(heads):
        load_g[h].wait()
        g_t[:, spans[h]] = g_rows[tiles[h]].T
    load_v.wait()
    values.got(4)
    value_tile(early[0])
    keys.got(6)
    for d in early[1:4]:
        keys.wait(d, lax.rem(d, 2) == 1)
        tops = score(d, tops)
    values.got(6)
    for d in early[4:]:
        keys.wait(d, lax.rem(d, 2) == 1)
        tops = score(d, tops)
    sums = None
    for d in early:
        sums = lift(d, tops, sums)
    for d in early[1:]:
        values.wait(d, lax.rem(d, 2) == 1)
        value_tile(d)

    keys.got_last()
    late = score(last, tops)
    late_sums = lift(last, late, None)
    values.got_last()
    value_tile(last)
    early_norm, late_norm = [], []
    for at in range(len(chunks)):
        fade = jnp.exp2((tops[at] - late[at]) * rate)
        norm = 1.0 / (sums[at] * fade + late_sums[at])
        early_norm.append(fade * norm)
        late_norm.append(norm)

    half = SLOTS // 2
    groups = (BACK[:half], BACK[half:])

    def deliver(back, group, grads):
        for at, d in enumerate(group):
            tile = grads[at * rows : (at + 1) * rows]
            if d % 2 == 1:
                back.send[d] = tile.astype(jnp.bfloat16)
                back.give(d)
            else:
                back.part[d] = tile

    def norms(d, at):
        return jnp.where(d == last, late_norm[at], early_norm[at]) if d else early_norm[at]

    for number, group in enumerate(groups):
        base = number * half * rows
        for at, d in enumerate(group):
            for c, cols in enumerate(chunks):
                weights = s_ref[d, :, cols] * norms(d, c)
                p_bf[base + at * rows : base + (at + 1) * rows, cols] = weights.astype(jnp.bfloat16)
        deliver(back_v, group, dot(p_bf[base : base + half * rows, :], g_rows[...]))

    deltas = []
    for cols in chunks:
        rounded = dot(v_t[...], p_bf[:, cols]).astype(jnp.bfloat16).astype(jnp.float32)
        o_t[:, cols] = rounded
        deltas.append(jnp.sum(rounded * g_t[:, cols].astype(jnp.float32), axis=0, keepdims=True))

    for number, group in enumerate(groups):
        base = number * half * rows
        for at, d in enumerate(group):
            for c, cols in enumerate(chunks):
                change = s_ref[d, :, cols] * ((dp_ref[d, :, cols] - deltas[c]) * (norms(d, c) * score_scale))
                ds_bf[base + at * rows : base + (at + 1) * rows, cols] = change.astype(jnp.bfloat16)
        deliver(back_k, group, dot(ds_bf[base : base + half * rows, :], q_rows[...]))

    def store(src, dst, at):
        copy = pltpu.make_async_copy(src, dst, store_sem.at[at])
        copy.start()
        return copy

    for d in (6, 4, 2):
        back_k.relay(d)
    for d in (6, 4, 2):
        back_v.relay(d)
    for h in range(heads):
        att[:, spans[h]] = o_t[:, h * rows : (h + 1) * rows].T.astype(jnp.bfloat16)
    stores = [store(att, att_out, 0)]
    for cols in chunks:
        grads = dot(k_t[...], ds_bf[:, cols])
        for at in range(CHUNK // rows):
            h = cols.start // rows + at
            dq[:, spans[h]] = grads[:, at * rows : (at + 1) * rows].T.astype(jnp.bfloat16)
    stores.append(store(dq, dq_out, 1))
    back_v.final()
    stores.append(store(out_v, dv_out, 2))
    back_k.final()
    stores.append(store(out_k, dk_out, 3))
    for part in (keys, values, back_v, back_k):
        part.finish()
    for copy in stores:
        copy.wait()


def hand_on(*refs):
    sources, results, staged, sems = refs[:4], refs[4:8], refs[8:12], refs[12]
    pieces = []
    for source, result, stage in zip(sources, results, staged):
        half = source.shape[0] // 2
        for at in (pl.ds(0, half), pl.ds(half, half)):
            pieces.append((source.at[at], stage.at[at], result.at[at]))
    reads = [pltpu.make_async_copy(p[0], p[1], sems.at[0, at]) for at, p in enumerate(pieces)]
    writes = [pltpu.make_async_copy(p[1], p[2], sems.at[1, at]) for at, p in enumerate(pieces)]
    for read in reads:
        read.start()
    for read, write in zip(reads, writes):
        read.wait()
        write.start()
    for write in writes:
        write.wait()


def local(queries, key_rows, value_rows, out_grad, doc_blocks):
    rows, width = key_rows.shape
    heads = queries.shape[1] // width
    total = rows * heads
    span = SLOTS * rows
    bf, f32 = jnp.bfloat16, jnp.float32
    blocks = pltpu.VMEM((SLOTS, rows, width), bf)
    dma = pltpu.SemaphoreType.DMA
    anywhere = pl.BlockSpec(memory_space=pl.ANY)
    scratch = [
        blocks, blocks,
        pltpu.VMEM((total, width), bf), pltpu.VMEM((total, width), bf),
        pltpu.VMEM((width, total), bf), pltpu.VMEM((width, total), bf),
        pltpu.VMEM((width, span), bf), pltpu.VMEM((width, span), bf),
        pltpu.VMEM((SLOTS, rows, total), f32), pltpu.VMEM((SLOTS, rows, total), f32),
        pltpu.VMEM((span, total), bf), pltpu.VMEM((span, total), bf),
        pltpu.VMEM((width, total), f32),
        pltpu.VMEM((rows, heads * width), bf), pltpu.VMEM((rows, heads * width), bf),
        pltpu.VMEM((SLOTS, rows, width), f32), pltpu.VMEM((SLOTS, rows, width), f32),
        blocks, blocks,
        blocks, blocks,
        pltpu.VMEM((4, rows, width), bf), pltpu.VMEM((4, rows, width), bf),
        pltpu.VMEM((rows, width), bf), pltpu.VMEM((rows, width), bf),
        pltpu.SMEM(doc_blocks.shape, jnp.int32),
        dma((3 + 2 * heads,)), dma((4,)),
        dma((11,)), dma((8,)), dma((11,)), dma((8,)),
        dma((8,)), dma((8,)), dma((4,)), dma((8,)), dma((8,)), dma((4,)),
    ]
    results = (
        jax.ShapeDtypeStruct(queries.shape, bf),
        jax.ShapeDtypeStruct(queries.shape, bf),
        jax.ShapeDtypeStruct(key_rows.shape, bf),
        jax.ShapeDtypeStruct(key_rows.shape, bf),
    )
    outputs = pl.pallas_call(
        kernel,
        out_shape=results,
        in_specs=[pl.BlockSpec(memory_space=pltpu.HBM)] * 4 + [anywhere],
        out_specs=(anywhere,) * 4,
        scratch_shapes=scratch,
        name="packed_attention",
        compiler_params=pltpu.CompilerParams(
            collective_id=0, has_side_effects=True
        ),
    )(queries, key_rows, value_rows, out_grad, doc_blocks)
    return pl.pallas_call(
        hand_on,
        out_shape=results,
        in_specs=[anywhere] * 4,
        out_specs=(anywhere,) * 4,
        scratch_shapes=[pltpu.VMEM(r.shape, r.dtype) for r in results] + [dma((2, 8))],
        name="hand_on",
    )(*outputs)


def solution(mesh):
    in_specs = (P("seq", "head"), P("seq", "head"), P("seq", "head"), P("seq", "head"), P())
    out_specs = (P("seq", "head"), P("seq", "head"), P("seq", "head"), P("seq", "head"))
    return jax.shard_map(local, mesh=mesh, in_specs=in_specs, out_specs=out_specs, check_vma=False)
```

time: 44.5 us -> 40.3 us (0.906)
  the two profiles are of different devices: /device:TPU:94 before, /device:TPU:774 now
where the time goes in v2:
time: 40.3 us; the launch traced here: 40.1 us
  Pallas kernels  39.5 us (98%)
  between operations  0.64 us (2%)
    pallas_call x1, Pallas kernels, local(): pl.pallas_call(kernel, out_shape=results, in_specs=[pl.BlockSpec(memory_s...  37.6 us
    pallas_call x1, Pallas kernels, local(): pl.pallas_call(hand_on, out_shape=results, in_specs=[anywhere] * 4, out_s...  1.9 us

profile of v2, /device:TPU:774, one launch (start us, length us, event | category | flops | bytes accessed | tf_op | source)
XLA Modules:
  0.0 40.1 jit_solution(167973272007903489)
XLA Ops:
  0.6 37.6 %packed_attention.1 = (bf16[128,1024]{1,0:T(8,128)(2,1)}, bf16[128,1024]{1,0:T(8,128)(2,1)}, bf16[128,128]{1,0:T(8,128)(2,1)}, bf16[128,128]{1,0:T(8,128)(2,1)}) custom-call(bf16[128,1024]{1,0:T(8,128)(2,1)} %q_hbm.1, bf16[128,128]{1,0:T(8,128)(2,1)} %k_hbm.1, bf16[128,128]{1,0:T(8,128)(2,1)} %v_hbm.1, bf16[128,1024]{1,0:T(8,128)(2,1)} %g_hbm.1, s32[64]{0:T(128)} %docs_hbm.1), custom_call_target="tpu_custom_call" | custom-call | tf_op jit(solution)/shard_map/packed_attention/pallas_call | solution.py:429
  38.2 1.9 %hand_on.1 = (bf16[128,1024]{1,0:T(8,128)(2,1)}, bf16[128,1024]{1,0:T(8,128)(2,1)}, bf16[128,128]{1,0:T(8,128)(2,1)}, bf16[128,128]{1,0:T(8,128)(2,1)}) custom-call(bf16[128,1024]{1,0:T(8,128)(2,1)} %get-tuple-element.8.refs_0_, bf16[128,1024]{1,0:T(8,128)(2,1)} %get-tuple-element.9.refs_1_, bf16[128,128]{1,0:T(8,128)(2,1)} %get-tuple-element.10.refs_2_, ...), custom_call_target="tpu_custom_call" | custom-call | tf_op jit(solution)/shard_map/hand_on/pallas_call | solution.py:440

commit v3 on v2

--- a/solution.py
+++ b/solution.py
@@ -124,8 +124,10 @@
                 self.push((me >= 5) & (odd == 1) & (me + 3 <= final_device), 4, 7, me + 3, 9)
             self.across(slot, slot // 2 + 1 if slot < 6 else 5, ready)
 
-        def got_last(self):
-            self.wait(last)
+        def got_last(self, when=True):
+            self.wait(last, when)
+
+        def last_across(self):
             self.push((me == 2) | (me == 4), last, last + 1, mate, 10)
 
         def finish(self):
@@ -150,7 +152,7 @@
         def give(self, d):
             slot = d + 1 - 2 * odd
             if d == 7:
-                self.push((me >= d) & even, d, self.far.at[3], self.far_sem.at[3], me - d)
+                self.push((me >= d) & even, d, self.far.at[3], self.far_sem.at[3], me - 3)
                 self.push((me >= d) & (odd == 1), d, self.mates.at[6], self.mate_sem.at[6], mate)
             else:
                 self.push(me >= d, d, self.mates.at[slot], self.mate_sem.at[slot], mate)
@@ -168,30 +170,43 @@
             ).wait_recv()
             return self.far[at].astype(jnp.float32)
 
-        def relay(self, d):
-            @pl.when(me >= d)
-            def _():
-                self.send[d] = (self.part[d] + self.wait_mate(d)).astype(jnp.bfloat16)
-                at = d // 2 - 1
+        def relay(self, d, when=True):
+            def send(at, device):
                 remote(
-                    self.send.at[d], self.far.at[at], self.send_sem.at[d], self.far_sem.at[at], me - d
+                    self.send.at[d], self.far.at[at], self.send_sem.at[d], self.far_sem.at[at], device
                 ).start()
 
-            self.sent.append(d)
+            @pl.when((me >= d) & when)
+            def _():
+                self.part[d] = self.part[d] + self.wait_mate(d)
+                if d == 4:
+                    @pl.when((me >= 6) & (me + 2 <= final_device))
+                    def _():
+                        self.part[d] = self.part[d] + self.wait_far(4)
+
+                    @pl.when((odd == 1) & (me >= 5) & (me + 3 <= final_device))
+                    def _():
+                        self.part[d] = self.part[d] + self.wait_far(3)
+
+                self.send[d] = self.part[d].astype(jnp.bfloat16)
+                if d == 6:
+                    pl.when(me >= SLOTS)(lambda: send(4, me - 2))
+                    pl.when(me < SLOTS)(lambda: send(2, me - 6))
+                else:
+                    send(d // 2 - 1, me - d)
+
+            if d not in self.sent:
+                self.sent.append(d)
 
         def final(self):
             @pl.when(even)
             def _():
                 self.part[0] = self.part[0] + self.wait_mate(0)
 
-            for at, steps in ((0, 2), (1, 4), (2, 6)):
-                @pl.when(me + steps <= final_device)
+            for at, steps, limit in ((0, 2, final_device), (1, 4, final_device), (2, 6, SLOTS - 1)):
+                @pl.when(me + steps <= limit)
                 def _():
                     self.part[0] = self.part[0] + self.wait_far(at)
-
-            @pl.when((odd == 1) & (me + 7 <= final_device))
-            def _():
-                self.part[0] = self.part[0] + self.wait_far(3)
 
             self.out[...] = self.part[0].astype(jnp.bfloat16)
 
@@ -293,15 +308,18 @@
     sums = None
     for d in early:
         sums = lift(d, tops, sums)
-    for d in early[1:]:
+    for d in early[1:4]:
         values.wait(d, lax.rem(d, 2) == 1)
         value_tile(d)
 
+    passes_on = (me == 2) | (me == 4)
+    outer = me < SLOTS
     keys.got_last()
+    keys.last_across()
     late = score(last, tops)
     late_sums = lift(last, late, None)
-    values.got_last()
-    value_tile(last)
+    values.got_last(passes_on)
+    values.last_across()
     early_norm, late_norm = [], []
     for at in range(len(chunks)):
         fade = jnp.exp2((tops[at] - late[at]) * rate)
@@ -332,6 +350,14 @@
                 p_bf[base + at * rows : base + (at + 1) * rows, cols] = weights.astype(jnp.bfloat16)
         deliver(back_v, group, dot(p_bf[base : base + half * rows, :], g_rows[...]))
 
+    for d in early[4:]:
+        values.wait(d, lax.rem(d, 2) == 1)
+        value_tile(d)
+    back_v.relay(6, me >= SLOTS)
+    back_v.relay(2, me >= SLOTS)
+    values.got_last(jnp.logical_not(passes_on))
+    value_tile(last)
+
     deltas = []
     for cols in chunks:
         rounded = dot(v_t[...], p_bf[:, cols]).astype(jnp.bfloat16).astype(jnp.float32)
@@ -351,10 +377,13 @@
         copy.start()
         return copy
 
+    back_k.relay(6)
+    back_v.relay(4, me >= SLOTS)
+    for d in (4, 2):
+        back_k.relay(d, outer)
     for d in (6, 4, 2):
-        back_k.relay(d)
-    for d in (6, 4, 2):
-        back_v.relay(d)
+        back_v.relay(d, outer)
+    back_k.relay(2, me >= SLOTS)
     for h in range(heads):
         att[:, spans[h]] = o_t[:, h * rows : (h + 1) * rows].T.astype(jnp.bfloat16)
     stores = [store(att, att_out, 0)]
@@ -364,6 +393,7 @@
             h = cols.start // rows + at
             dq[:, spans[h]] = grads[:, at * rows : (at + 1) * rows].T.astype(jnp.bfloat16)
     stores.append(store(dq, dq_out, 1))
+    back_k.relay(4, me >= SLOTS)
     back_v.final()
     stores.append(store(out_v, dv_out, 2))
     back_k.final()
@@ -413,12 +443,12 @@
         pltpu.VMEM((SLOTS, rows, width), f32), pltpu.VMEM((SLOTS, rows, width), f32),
         blocks, blocks,
         blocks, blocks,
-        pltpu.VMEM((4, rows, width), bf), pltpu.VMEM((4, rows, width), bf),
+        pltpu.VMEM((5, rows, width), bf), pltpu.VMEM((5, rows, width), bf),
         pltpu.VMEM((rows, width), bf), pltpu.VMEM((rows, width), bf),
         pltpu.SMEM(doc_blocks.shape, jnp.int32),
         dma((3 + 2 * heads,)), dma((4,)),
         dma((11,)), dma((8,)), dma((11,)), dma((8,)),
-        dma((8,)), dma((8,)), dma((4,)), dma((8,)), dma((8,)), dma((4,)),
+        dma((8,)), dma((8,)), dma((5,)), dma((8,)), dma((8,)), dma((5,)),
     ]
     results = (
         jax.ShapeDtypeStruct(queries.shape, bf),

time: 40.3 us -> 39.4 us (0.978)
  the two profiles are of different devices: /device:TPU:774 before, /device:TPU:1 now
where the time goes in v3:
time: 39.4 us; the launch traced here: 39.2 us
  Pallas kernels  38.6 us (98%)
  between operations  0.64 us (2%)
    pallas_call x1, Pallas kernels, local(): pl.pallas_call(kernel, out_shape=results, in_specs=[pl.BlockSpec(memory_s...  36.7 us
    pallas_call x1, Pallas kernels, local(): pl.pallas_call(hand_on, out_shape=results, in_specs=[anywhere] * 4, out_s...  1.9 us

profile of v3, /device:TPU:1, one launch (start us, length us, event | category | flops | bytes accessed | tf_op | source)
XLA Modules:
  0.0 39.2 jit_solution(15587461082929544417)
XLA Ops:
  0.6 36.7 %packed_attention.1 = (bf16[128,1024]{1,0:T(8,128)(2,1)}, bf16[128,1024]{1,0:T(8,128)(2,1)}, bf16[128,128]{1,0:T(8,128)(2,1)}, bf16[128,128]{1,0:T(8,128)(2,1)}) custom-call(bf16[128,1024]{1,0:T(8,128)(2,1)} %q_hbm.1, bf16[128,128]{1,0:T(8,128)(2,1)} %k_hbm.1, bf16[128,128]{1,0:T(8,128)(2,1)} %v_hbm.1, bf16[128,1024]{1,0:T(8,128)(2,1)} %g_hbm.1, s32[64]{0:T(128)} %docs_hbm.1), custom_call_target="tpu_custom_call" | custom-call | tf_op jit(solution)/shard_map/packed_attention/pallas_call | solution.py:459
  37.3 1.9 %hand_on.1 = (bf16[128,1024]{1,0:T(8,128)(2,1)}, bf16[128,1024]{1,0:T(8,128)(2,1)}, bf16[128,128]{1,0:T(8,128)(2,1)}, bf16[128,128]{1,0:T(8,128)(2,1)}) custom-call(bf16[128,1024]{1,0:T(8,128)(2,1)} %get-tuple-element.8.refs_0_, bf16[128,1024]{1,0:T(8,128)(2,1)} %get-tuple-element.9.refs_1_, bf16[128,128]{1,0:T(8,128)(2,1)} %get-tuple-element.10.refs_2_, ...), custom_call_target="tpu_custom_call" | custom-call | tf_op jit(solution)/shard_map/hand_on/pallas_call | solution.py:470
